TPU v7x, 32 devices: a whole 2x2x4 slice. The times are simulated.
32 devices in a mesh: groups: 2 (over y), seq: 4 (over z), mp: 2 (over x), enc: 2 (over core).
Axes of the slice: x: 2, y: 2, z: 4, core: 2. Of those that a mesh axis runs over, the one named last changes fastest.
Arguments:
- tokens: bfloat16 [4096, 4096], P(('groups', 'seq'), ('mp', 'enc')), parts along dimension 0, may hold values from -6 to 6
- nbr_feats: bfloat16 [192, 128, 4096], P(('groups', 'seq'), None, ('mp', 'enc')), parts along dimension 0, may hold values from -6 to 6
- counts: int32 [8], P('groups'), parts along dimension 0, may hold values from 8 to 24, as said below
- slot_target: int32 [192], P(('groups', 'seq')), parts along dimension 0, may hold values from 0 to 63, as said below
- w_query: bfloat16 [4096, 512], P(None, ('mp', 'enc')), may hold values from -32 to 32
- w_keyval: bfloat16 [4096, 512], P(None, ('mp', 'enc')), may hold values from -1 to 1
Outputs:
- attended: bfloat16 [4096, 512], P(('groups', 'seq'), ('mp', 'enc')), parts along dimension 0
There are 2 independent parts, one for each index of `groups`. A program takes and returns all parts, laid end to end along the dimension named above; an argument that names none is the same for every part. Nothing has to cross between parts.
Inputs may be any that keep to these rules, and one draw needn't show every extreme that they name: Each seq index's live slots are its first counts slots; the counts sum to 64. `slot_target`: A live slot holds neighbour o * 16 + l of the spans of seq index o; every neighbour is held by exactly one live slot; the live slots of one seq index hold at most 8 neighbours of any one seq index; dead slots hold arbitrary values of the range.
All inputs are finite; a program needn't handle non-finite values.
Results may differ from a plain program's by a relative error of at most 0.003.
The roundings to bfloat16 on the way count: a program that leaves them out, or rounds other values in their place, can miss the bound.
Values may be sent and summed in bfloat16 or wider, within the bound.
A program may use at most 128 MiB of HBM per device.

v0:
```python
import jax
import jax.numpy as jnp
from jax import lax
from jax.sharding import PartitionSpec as P

D = 4096
SPAN = 64
NBR = 2
RLEN = 128
CH_SEQ = 8
NB_SEQ = 16
ENC_CAP = 24
epsilon = 1e-05


def partner_2(block, axis, stride):
    count = lax.axis_size(axis)
    route = []
    for low in range(count):
        high = low | 1 << stride
        if high != low and high < count:
            route += [(low, high), (high, low)]
    return lax.ppermute(block, axis, route)


def passed_along(block, axis, distance):
    devices = range(lax.axis_size(axis))
    route = [(i - distance, i) for i in devices if i - distance in devices]
    return lax.ppermute(block, axis, route)


def project_fold(weight, piece):
    width = piece.shape[-1]
    flat_rows = piece.reshape(-1, width)
    running = jnp.dot(flat_rows, weight, preferred_element_type=jnp.float32)
    widened = flat_rows.astype(jnp.float32)
    squares = jnp.sum(widened * widened, axis=1)
    return (running, squares)


def normalized(carry, factor):
    running, squares = carry
    scale_rows = lax.rsqrt(squares / D + epsilon) * factor
    return (running * scale_rows[:, None]).astype(jnp.bfloat16)


def routing_plan(slot_target, counts, pair_cap):
    seq_count = counts.shape[0]
    seq_here = lax.axis_index("seq")
    live_count = jnp.sum(jnp.where(jnp.arange(seq_count) == seq_here, counts, 0))
    slot_ids = jnp.arange(ENC_CAP)
    live_slots = slot_ids < live_count
    owner_of = slot_target // NB_SEQ
    position = slot_target % NB_SEQ
    same_owner = (
        (owner_of[:, None] == owner_of[None, :])
        & live_slots[None, :]
        & (slot_ids[None, :] < slot_ids[:, None])
    )
    rank_within = jnp.sum(same_owner.astype(jnp.int32), axis=1)
    target_slot = owner_of * pair_cap + rank_within
    buffer_ids = jnp.arange(seq_count * pair_cap)
    chosen = (buffer_ids[:, None] == target_slot[None, :]) & live_slots[None, :]
    sent_ids = jnp.sum(jnp.where(chosen, position[None, :] + 1, 0), axis=1) - 1
    return (chosen, sent_ids.reshape(seq_count, pair_cap))


def pack_rows(chosen, payload, seq_count, pair_cap):
    packed = jnp.dot(chosen.astype(jnp.bfloat16), payload, preferred_element_type=jnp.float32)
    return packed.astype(jnp.bfloat16).reshape(seq_count, pair_cap, payload.shape[1])


def place_rows(received, received_ids):
    flat_rows = received.reshape(-1, received.shape[-1])
    picker = received_ids.reshape(1, -1) == jnp.arange(NB_SEQ)[:, None]
    placed = jnp.dot(picker.astype(jnp.bfloat16), flat_rows, preferred_element_type=jnp.float32)
    return placed.astype(jnp.bfloat16)


def local(tokens, nbr_feats, counts, slot_target, w_query, w_keyval):
    seq_count = lax.axis_size("seq")
    pair_cap = max(2, 2 * NB_SEQ // seq_count)
    head_size = w_keyval.shape[1]
    chosen, sent_ids = routing_plan(slot_target, counts, pair_cap)
    folded = project_fold(w_keyval, lax.all_gather(nbr_feats, ("mp", "enc"), axis=2, tiled=True))
    encoded = normalized(folded, 1.0).reshape(ENC_CAP, RLEN * head_size)
    packed = pack_rows(chosen, encoded, seq_count, pair_cap)
    received, received_ids = (
        lax.all_to_all(packed, "seq", split_axis=0, concat_axis=0, tiled=True),
        lax.all_to_all(sent_ids, "seq", split_axis=0, concat_axis=0, tiled=True),
    )
    own_half = place_rows(received, received_ids).reshape(NB_SEQ, RLEN, head_size)
    partner = partner_2(own_half, "enc", 0)
    first_lane = lax.axis_index("enc") == 0
    key_rows = jnp.where(first_lane, own_half, partner).reshape(CH_SEQ, NBR * RLEN, head_size)
    value_rows = jnp.where(first_lane, partner, own_half).reshape(CH_SEQ, NBR * RLEN, head_size)
    prior_keys, prior_values = passed_along((key_rows[-1], value_rows[-1]), "seq", 1)
    context_keys = jnp.concatenate([prior_keys[None], key_rows[:-1]], axis=0)
    context_values = jnp.concatenate([prior_values[None], value_rows[:-1]], axis=0)
    folded_tokens = project_fold(w_query, lax.all_gather(tokens, ("mp", "enc"), axis=1, tiled=True))
    queries = normalized(folded_tokens, head_size ** (-0.5)).reshape(CH_SEQ, SPAN, head_size)
    scores = jnp.einsum("cqd,ckd->cqk", queries, context_keys, preferred_element_type=jnp.float32)
    weights = jax.nn.softmax(scores, axis=-1).astype(jnp.bfloat16)
    attended = jnp.einsum(
        "cqk,ckd->cqd", weights, context_values, preferred_element_type=jnp.float32
    )
    return attended.astype(jnp.bfloat16).reshape(CH_SEQ * SPAN, head_size)


def solution(mesh):
    placed = (
        P(("groups", "seq"), ("mp", "enc")),
        P(("groups", "seq"), None, ("mp", "enc")),
        P("groups"),
        P(("groups", "seq")),
        P(None, ("mp", "enc")),
        P(None, ("mp", "enc")),
    )
    return jax.shard_map(
        local,
        mesh=mesh,
        in_specs=placed,
        out_specs=P(("groups", "seq"), ("mp", "enc")),
        check_vma=False,
    )
```

profile of v0, /device:TPU:16, one launch (start us, length us, event | category | flops | bytes accessed | tf_op | source)
XLA Modules:
  0.0 241.7 jit_solution(9443308790571083364)
XLA Ops:
  6.5 0.0 copy-start
  6.5 0.0 copy-start.3
  6.5 0.0 copy-start.4
  6.5 0.0 all-gather.5.cloned.1.call-start
  6.5 0.7 all-gather.5.cloned.1.call-update
  7.3 0.0 all-gather.3.cloned.1.call-start
  7.3 0.7 all-gather.3.cloned.1.call-update
  8.0 0.0 copy-done.3
  8.0 0.0 copy-done.4
  8.1 0.6 fusion.24
  8.7 0.6 iota_compare_fusion.4
  9.3 0.2 convert_reduce_fusion
  9.5 0.1 select_reduce_fusion
  9.6 0.7 sub.20
  10.3 5.2 %all-to-all-start = ((s32[4,1,8]{2,1,0:T(1,128)}), s32[4,1,8]{2,1,0:T(1,128)S(1)}, u32[]{:S(2)}, u32[]{:S(2)}) async-start(s32[4,1,8]{2,1,0:T(1,128)} %bitcast.1), calls=%async_computation | async-start | bytes 4096 | tf_op jit(solution)/shard_map/all_to_all | solution.py:90
  15.5 149.4 %all-gather.5.cloned.1.call-done = bf16[24,128,4096]{2,1,0:T(8,128)(2,1)} async-done(((bf16[24,128,1024]{2,1,0:T(8,128)(2,1)}), bf16[24,128,4096]{2,1,0:T(8,128)(2,1)}) %all-gather.5.cloned.1.call-update) | async-done | bytes 25165840 | tf_op jit(solution)/shard_map/all_gather | solution.py:85
  164.9 10.6 %multiply_reduce_fusion = f32[24,128]{1,0:T(8,128)S(1)} fusion(bf16[24,128,4096]{2,1,0:T(8,128)(2,1)} %all-gather.5.cloned.1.call-done), kind=kLoop, calls=%fused_computation.1 | loop fusion | flops 37745664 | bytes 25178112 | tf_op jit(solution)/shard_map/reduce_sum | solution.py:37
  175.6 0.0 copy-done
  175.6 12.0 %fusion.2 = bf16[3072,128]{1,0:T(8,128)(2,1)S(1)} fusion(bf16[3072,4096]{1,0:T(8,128)(2,1)} %bitcast.30, bf16[4096,128]{1,0:T(8,128)(2,1)S(1)} %copy-done, f32[3072]{0:T(1024)S(1)} %rsqrt_bitcast_fusion), kind=kOutput, calls=%fused_computation.7 | convolution fusion | flops 3222011904 | bytes 27013120 | tf_op jit(solution)/shard_map/dot_general | solution.py:35
  187.6 0.3 reshape.81
  188.0 1.5 fusion.1
  189.5 0.0 all-to-all-done
  189.5 5.1 %all-to-all-start.1 = ((bf16[4,8,16384]{2,1,0:T(8,128)(2,1)}), bf16[4,8,16384]{2,1,0:T(8,128)(2,1)S(1)}, u32[]{:S(2)}, u32[]{:S(2)}) async-start(bf16[4,8,16384]{2,1,0:T(8,128)(2,1)} %fusion.1), calls=%async_computation.1 | async-start | bytes 2097152 | tf_op jit(solution)/shard_map/all_to_all | solution.py:89
  194.6 0.5 broadcast.93
  195.1 0.7 reduce.4
  195.8 0.1 eq.61
  195.9 21.7 %all-to-all-done.1 = bf16[4,8,16384]{2,1,0:T(8,128)(2,1)S(1)} async-done(((bf16[4,8,16384]{2,1,0:T(8,128)(2,1)}), bf16[4,8,16384]{2,1,0:T(8,128)(2,1)S(1)}, u32[]{:S(2)}, u32[]{:S(2)}) %all-to-all-start.1) | async-done | bytes 1048608 | tf_op jit(solution)/shard_map/all_to_all | solution.py:89
  217.6 0.3 fusion.4
  217.8 0.1 copy.9
  217.9 0.1 collective-permute-start
  218.0 0.0 all-gather.3.cloned.1.call-done
  218.0 0.0 copy-start.1
  218.1 0.0 copy-start.2
  218.1 3.2 %multiply_reduce_fusion.1 = f32[512]{0:T(512)S(1)} fusion(bf16[512,4096]{1,0:T(8,128)(2,1)} %all-gather.3.cloned.1.call-done), kind=kLoop, calls=%fused_computation.5 | loop fusion | flops 6290944 | bytes 4196352 | tf_op jit(solution)/shard_map/reduce_sum | solution.py:37
  221.3 0.0 collective-permute-done
  221.3 0.1 broadcast_select_fusion.1
  221.5 4.3 %collective-permute-start.1 = (bf16[256,128]{1,0:T(8,128)(2,1)S(1)}, bf16[256,128]{1,0:T(8,128)(2,1)S(1)}, u32[]{:S(2)}, u32[]{:S(2)}) collective-permute-start(bf16[256,128]{1,0:T(8,128)(2,1)S(1)} %bitcast.39), channel_id=1, source_target_pairs={{0,4},{4,8},{8,12},{1,5},{5,9},{9,13},{2,6},{6,10},{10,14},{3,7},{... | collective-permute-start | bytes 196616 | tf_op jit(solution)/shard_map/ppermute | solution.py:29
  225.7 0.0 copy-done.1
  225.8 0.0 copy-done.2
  225.8 1.3 fusion.6
  227.1 1.9 collective-permute-start.2
  229.0 0.0 collective-permute-done.1
  229.1 0.3 fusion.8
  229.4 0.5 fusion.31
  229.8 3.4 %collective-permute-done.2 = bf16[256,128]{1,0:T(8,128)(2,1)S(1)} collective-permute-done((bf16[256,128]{1,0:T(8,128)(2,1)S(1)}, bf16[256,128]{1,0:T(8,128)(2,1)S(1)}, u32[]{:S(2)}, u32[]{:S(2)}) %collective-permute-start.2) | collective-permute-done | bytes 65568 | tf_op jit(solution)/shard_map/ppermute | solution.py:29
  233.3 1.6 convolution_convert_fusion.2
  (9 shorter events, 0.1 us)
Async XLA Ops:
  6.5 169.0 %copy-start = (bf16[4096,128]{1,0:T(8,128)(2,1)S(1)}, bf16[4096,128]{1,0:T(8,128)(2,1)}, u32[]{:S(2)}) copy-start(bf16[4096,128]{1,0:T(8,128)(2,1)} %param.11) | copy-start | bytes 3145732
  6.5 1.5 copy-start.3
  6.5 1.5 copy-start.4
  6.5 158.4 %all-gather.5.cloned.1.call-start = ((), (), s32[]{:S(2)}) async-start(), calls=%async_computation.3 | async-start | bytes 31457280 | tf_op jit(solution)/shard_map/all_gather | solution.py:85
  7.3 210.8 %all-gather.3.cloned.1.call-start = ((), (), s32[]{:S(2)}) async-start(), calls=%async_computation.2 | async-start | bytes 5242880 | tf_op jit(solution)/shard_map/all_gather | solution.py:100
  10.3 179.2 %all-to-all-start = ((s32[4,1,8]{2,1,0:T(1,128)}), s32[4,1,8]{2,1,0:T(1,128)S(1)}, u32[]{:S(2)}, u32[]{:S(2)}) async-start(s32[4,1,8]{2,1,0:T(1,128)} %bitcast.1), calls=%async_computation | async-start | bytes 4096 | tf_op jit(solution)/shard_map/all_to_all | solution.py:90
  189.5 28.0 %all-to-all-start.1 = ((bf16[4,8,16384]{2,1,0:T(8,128)(2,1)}), bf16[4,8,16384]{2,1,0:T(8,128)(2,1)S(1)}, u32[]{:S(2)}, u32[]{:S(2)}) async-start(bf16[4,8,16384]{2,1,0:T(8,128)(2,1)} %fusion.1), calls=%async_computation.1 | async-start | bytes 2097152 | tf_op jit(solution)/shard_map/all_to_all | solution.py:89
  217.9 3.4 %collective-permute-start = (bf16[16,128,128]{2,1,0:T(8,128)(2,1)S(1)}, bf16[16,128,128]{2,1,0:T(8,128)(2,1)S(1)}, u32[]{:S(2)}, u32[]{:S(2)}) collective-permute-start(bf16[16,128,128]{2,1,0:T(8,128)(2,1)S(1)} %bitcast.31), channel_id=1, source_target_pairs={{0,1},{1,0},{2,3},{3,2},{4,5},{5,4},{6,7},{7,6},{8,9},{9,8},{10,11... | collective-permute-start | bytes 1572872 | tf_op jit(solution)/shard_map/ppermute | solution.py:23
  218.0 7.7 %copy-start.1 = (bf16[512,4096]{1,0:T(8,128)(2,1)S(1)}, bf16[512,4096]{1,0:T(8,128)(2,1)}, u32[]{:S(2)}) copy-start(bf16[512,4096]{1,0:T(8,128)(2,1)} %all-gather.3.cloned.1.call-done) | copy-start | bytes 12582916
  218.1 7.7 %copy-start.2 = (bf16[4096,128]{1,0:T(8,128)(2,1)S(1)}, bf16[4096,128]{1,0:T(8,128)(2,1)}, u32[]{:S(2)}) copy-start(bf16[4096,128]{1,0:T(8,128)(2,1)} %param.10) | copy-start | bytes 3145732
  221.5 7.6 %collective-permute-start.1 = (bf16[256,128]{1,0:T(8,128)(2,1)S(1)}, bf16[256,128]{1,0:T(8,128)(2,1)S(1)}, u32[]{:S(2)}, u32[]{:S(2)}) collective-permute-start(bf16[256,128]{1,0:T(8,128)(2,1)S(1)} %bitcast.39), channel_id=1, source_target_pairs={{0,4},{4,8},{8,12},{1,5},{5,9},{9,13},{2,6},{6,10},{10,14},{3,7},{... | collective-permute-start | bytes 196616 | tf_op jit(solution)/shard_map/ppermute | solution.py:29
  227.1 6.2 %collective-permute-start.2 = (bf16[256,128]{1,0:T(8,128)(2,1)S(1)}, bf16[256,128]{1,0:T(8,128)(2,1)S(1)}, u32[]{:S(2)}, u32[]{:S(2)}) collective-permute-start(bf16[256,128]{1,0:T(8,128)(2,1)S(1)} %bitcast.40), channel_id=1, source_target_pairs={{0,4},{4,8},{8,12},{1,5},{5,9},{9,13},{2,6},{6,10},{10,14},{3,7},{... | collective-permute-start | bytes 196616 | tf_op jit(solution)/shard_map/ppermute | solution.py:29
Sparse Core Ops, SparseCore 0:
  8.9 155.9 all-gather.4
  166.5 34.4 all-gather.2
where the time goes:
time: 242 us
  waiting for transfers between devices  176 us (73%)
  matrix products  17.5 us (7%)
  starting transfers between devices  16.6 us (7%)
  other arithmetic  16.3 us (7%)
  between operations  13.6 us (6%)
    all_gather x1, waiting for transfers between devices, local(): lax.all_gather(nbr_feats, ('mp', 'enc'), axis=2, tiled=True)  149 us
    all_to_all x1, waiting for transfers between devices, local(): lax.all_to_all(packed, 'seq', split_axis=0, concat_axis=0, tiled=True)  21.7 us
    reduce_sum x2, other arithmetic, project_fold(): squares = jnp.sum(widened * widened, axis=1)  13.9 us
    dot_general x2, matrix products, project_fold(): running = jnp.dot(flat_rows, weight, preferred_element_type=jnp.float32)  13.3 us
    ppermute x2, starting transfers between devices, passed_along(): return lax.ppermute(block, axis, route)  6.2 us
    all_to_all x1, starting transfers between devices, local(): lax.all_to_all(sent_ids, 'seq', split_axis=0, concat_axis=0, tiled=True)  5.2 us
    all_to_all x1, starting transfers between devices, local(): lax.all_to_all(packed, 'seq', split_axis=0, concat_axis=0, tiled=True)  5.11 us
  transfers between devices with their start and end apart: 7, of which 3 were waited for; matrix products, arithmetic and copies ran while one was open for 14% of the time, Pallas kernels for 0%

commit v1 on v0

--- a/solution.py
+++ b/solution.py
@@ -11,6 +11,22 @@
 NB_SEQ = 16
 ENC_CAP = 24
 epsilon = 1e-05
+
+
+def exchange_in_pairs(x, axis, split, join):
+    ways, here = (lax.axis_size(axis), lax.axis_index(axis))
+    width = x.shape[split] // ways
+    shape = list(x.shape)
+    shape[split] = width
+    height = shape[join]
+    shape[join] = height * ways
+    full = jnp.zeros(shape, x.dtype)
+    for mask in range(ways):
+        part = lax.dynamic_slice_in_dim(x, (here ^ mask) * width, width, axis=split)
+        if mask:
+            part = lax.ppermute(part, axis, [(d, d ^ mask) for d in range(ways)])
+        full = lax.dynamic_update_slice_in_dim(full, part, (here ^ mask) * height, axis=join)
+    return full
 
 
 def partner_2(block, axis, stride):
@@ -86,7 +102,7 @@
     encoded = normalized(folded, 1.0).reshape(ENC_CAP, RLEN * head_size)
     packed = pack_rows(chosen, encoded, seq_count, pair_cap)
     received, received_ids = (
-        lax.all_to_all(packed, "seq", split_axis=0, concat_axis=0, tiled=True),
+        exchange_in_pairs(packed, "seq", 0, 0),
         lax.all_to_all(sent_ids, "seq", split_axis=0, concat_axis=0, tiled=True),
     )
     own_half = place_rows(received, received_ids).reshape(NB_SEQ, RLEN, head_size)

time: 242 us -> 248 us (1.025)
  waiting for transfers between devices: 176 us -> 186 us
  starting transfers between devices: 16.6 us -> 12 us
    ppermute x0 -> x3, waiting for transfers between devices: none -> 22.1 us  [exchange_in_pairs(): part = lax.ppermute(part, axis, [(d, d ^ mask) for d in range(ways)])]
    all_to_all x1 -> x0, waiting for transfers between devices: 21.7 us -> none  [local(): lax.all_to_all(packed, 'seq', split_axis=0, concat_axis=0, tiled=True)]
    all_gather x1, waiting for transfers between devices: 149 us -> 155 us  [local(): lax.all_gather(nbr_feats, ('mp', 'enc'), axis=2, tiled=True)]
    all_to_all x1 -> x0, starting transfers between devices: 5.11 us -> none  [local(): lax.all_to_all(packed, 'seq', split_axis=0, concat_axis=0, tiled=True)]
    ppermute x0 -> x3, starting transfers between devices: none -> 3.9 us  [exchange_in_pairs(): part = lax.ppermute(part, axis, [(d, d ^ mask) for d in range(ways)])]
    all_to_all x1, waiting for transfers between devices: 0.01 us -> 3.12 us  [local(): lax.all_to_all(sent_ids, 'seq', split_axis=0, concat_axis=0, tiled=True)]
  transfers between devices with their start and end apart: 7 -> 9, of which waited for: 3 -> 6; matrix products, arithmetic and copies ran while one was open for 14% -> 13% of each run, Pallas kernels for 0% -> 0%
where the time goes in v1:
time: 248 us; the launch traced here: 246 us
  waiting for transfers between devices  186 us (75%)
  matrix products  16.5 us (7%)
  other arithmetic  16.2 us (7%)
  between operations  13.7 us (6%)
  starting transfers between devices  12 us (5%)
    all_gather x1, waiting for transfers between devices, local(): lax.all_gather(nbr_feats, ('mp', 'enc'), axis=2, tiled=True)  155 us
    ppermute x3, waiting for transfers between devices, exchange_in_pairs(): part = lax.ppermute(part, axis, [(d, d ^ mask) for d in range(ways)])  22.1 us
    reduce_sum x2, other arithmetic, project_fold(): squares = jnp.sum(widened * widened, axis=1)  13.9 us
    dot_general x2, matrix products, project_fold(): running = jnp.dot(flat_rows, weight, preferred_element_type=jnp.float32)  13.3 us
  transfers between devices with their start and end apart: 9, of which 6 were waited for; matrix products, arithmetic and copies ran while one was open for 13% of the time, Pallas kernels for 0%

profile of v1, /device:TPU:16, one launch (start us, length us, event | category | flops | bytes accessed | tf_op | source)
XLA Modules:
  0.0 246.1 jit_solution(14546573068263089600)
XLA Ops:
  6.5 0.0 copy-start
  6.5 0.0 copy-start.3
  6.5 0.0 copy-start.4
  6.5 0.0 all-gather.5.cloned.1.call-start
  6.5 0.7 all-gather.5.cloned.1.call-update
  7.3 0.0 all-gather.3.cloned.1.call-start
  7.3 0.7 all-gather.3.cloned.1.call-update
  8.0 0.0 copy-done.3
  8.1 0.0 copy-done.4
  8.1 0.6 fusion.24
  8.7 0.6 iota_compare_fusion.4
  9.4 0.2 convert_reduce_fusion
  9.6 155.3 %all-gather.5.cloned.1.call-done = bf16[24,128,4096]{2,1,0:T(8,128)(2,1)} async-done(((bf16[24,128,1024]{2,1,0:T(8,128)(2,1)}), bf16[24,128,4096]{2,1,0:T(8,128)(2,1)}) %all-gather.5.cloned.1.call-update) | async-done | bytes 25165840 | tf_op jit(solution)/shard_map/all_gather | solution.py:101
  164.9 10.6 %multiply_reduce_fusion = f32[24,128]{1,0:T(8,128)S(1)} fusion(bf16[24,128,4096]{2,1,0:T(8,128)(2,1)} %all-gather.5.cloned.1.call-done), kind=kLoop, calls=%fused_computation.1 | loop fusion | flops 37745664 | bytes 25178112 | tf_op jit(solution)/shard_map/reduce_sum | solution.py:53
  175.5 0.0 copy-done
  175.5 12.0 %fusion.2 = bf16[3072,128]{1,0:T(8,128)(2,1)S(1)} fusion(bf16[3072,4096]{1,0:T(8,128)(2,1)} %bitcast.30, bf16[4096,128]{1,0:T(8,128)(2,1)S(1)} %copy-done, f32[3072]{0:T(1024)S(1)} %rsqrt_bitcast_fusion), kind=kOutput, calls=%fused_computation.7 | convolution fusion | flops 3222011904 | bytes 27013120 | tf_op jit(solution)/shard_map/dot_general | solution.py:51
  187.6 0.3 reshape.81
  187.9 0.6 fusion.1
  188.5 0.1 broadcast_in_dim.25
  188.6 0.1 constant_dynamic-slice_fusion
  188.6 1.5 collective-permute-start
  190.2 0.1 select_reduce_fusion
  190.3 0.7 sub.20
  190.9 4.2 %all-to-all-start = ((s32[4,1,8]{2,1,0:T(1,128)}), s32[4,1,8]{2,1,0:T(1,128)S(1)}, u32[]{:S(2)}, u32[]{:S(2)}) async-start(s32[4,1,8]{2,1,0:T(1,128)} %bitcast.1), calls=%async_computation | async-start | bytes 4096 | tf_op jit(solution)/shard_map/all_to_all | solution.py:106
  195.1 3.1 %all-to-all-done = s32[4,1,8]{2,1,0:T(1,128)S(1)} async-done(((s32[4,1,8]{2,1,0:T(1,128)}), s32[4,1,8]{2,1,0:T(1,128)S(1)}, u32[]{:S(2)}, u32[]{:S(2)}) %all-to-all-start) | async-done | bytes 160 | tf_op jit(solution)/shard_map/all_to_all | solution.py:106
  198.3 0.5 broadcast.93
  198.8 0.7 reduce.4
  199.4 0.1 eq.61
  199.5 2.4 collective-permute-start.1
  201.9 0.0 collective-permute-start.2
  201.9 0.0 collective-permute-done
  201.9 15.7 %collective-permute-done.1 = bf16[1,8,16384]{2,1,0:T(8,128)(2,1)S(1)} collective-permute-done((bf16[1,8,16384]{2,1,0:T(8,128)(2,1)S(1)}, bf16[1,8,16384]{2,1,0:T(8,128)(2,1)S(1)}, u32[]{:S(2)}, u32[]{:S(2)}) %collective-permute-start.1) | collective-permute-done | bytes 262176 | tf_op jit(solution)/shard_map/ppermute | solution.py:27
  217.7 6.4 %collective-permute-done.2 = bf16[1,8,16384]{2,1,0:T(8,128)(2,1)S(1)} collective-permute-done((bf16[1,8,16384]{2,1,0:T(8,128)(2,1)S(1)}, bf16[1,8,16384]{2,1,0:T(8,128)(2,1)S(1)}, u32[]{:S(2)}, u32[]{:S(2)}) %collective-permute-start.2) | collective-permute-done | bytes 262176 | tf_op jit(solution)/shard_map/ppermute | solution.py:27
  224.1 0.3 fusion.4
  224.4 0.1 copy.9
  224.5 0.1 collective-permute-start.3
  224.5 0.0 all-gather.3.cloned.1.call-done
  224.6 0.0 copy-start.1
  224.6 0.0 copy-start.2
  224.6 3.2 %multiply_reduce_fusion.1 = f32[512]{0:T(512)S(1)} fusion(bf16[512,4096]{1,0:T(8,128)(2,1)} %all-gather.3.cloned.1.call-done), kind=kLoop, calls=%fused_computation.5 | loop fusion | flops 6290944 | bytes 4196352 | tf_op jit(solution)/shard_map/reduce_sum | solution.py:53
  227.8 0.0 collective-permute-done.3
  227.8 0.1 broadcast_select_fusion.1
  228.0 1.9 collective-permute-start.4
  229.9 0.0 copy-done.1
  229.9 0.0 copy-done.2
  229.9 1.3 fusion.6
  231.3 1.9 collective-permute-start.5
  233.2 1.1 collective-permute-done.4
  234.3 0.3 fusion.8
  234.6 0.5 fusion.31
  235.1 2.5 %collective-permute-done.5 = bf16[256,128]{1,0:T(8,128)(2,1)S(1)} collective-permute-done((bf16[256,128]{1,0:T(8,128)(2,1)S(1)}, bf16[256,128]{1,0:T(8,128)(2,1)S(1)}, u32[]{:S(2)}, u32[]{:S(2)}) %collective-permute-start.5) | collective-permute-done | bytes 65568 | tf_op jit(solution)/shard_map/ppermute | solution.py:45
  237.6 1.6 convolution_convert_fusion.2
  (12 shorter events, 0.2 us)
Async XLA Ops:
  6.5 169.0 %copy-start = (bf16[4096,128]{1,0:T(8,128)(2,1)S(1)}, bf16[4096,128]{1,0:T(8,128)(2,1)}, u32[]{:S(2)}) copy-start(bf16[4096,128]{1,0:T(8,128)(2,1)} %param.11) | copy-start | bytes 3145732
  6.5 1.5 copy-start.3
  6.5 1.5 copy-start.4
  6.5 158.3 %all-gather.5.cloned.1.call-start = ((), (), s32[]{:S(2)}) async-start(), calls=%async_computation.2 | async-start | bytes 31457280 | tf_op jit(solution)/shard_map/all_gather | solution.py:101
  7.3 217.3 %all-gather.3.cloned.1.call-start = ((), (), s32[]{:S(2)}) async-start(), calls=%async_computation.1 | async-start | bytes 5242880 | tf_op jit(solution)/shard_map/all_gather | solution.py:116
  188.6 13.2 %collective-permute-start = (bf16[1,8,16384]{2,1,0:T(8,128)(2,1)S(1)}, bf16[1,8,16384]{2,1,0:T(8,128)(2,1)S(1)}, u32[]{:S(2)}, u32[]{:S(2)}) collective-permute-start(bf16[1,8,16384]{2,1,0:T(8,128)(2,1)S(1)} %get-tuple-element.9), channel_id=1, source_target_pairs={{0,4},{4,0},{8,12},{12,8},{1,5},{5,1},{9,13},{13,9},{2,6},{6,2},{1... | collective-permute-start | bytes 786440 | tf_op jit(solution)/shard_map/ppermute | solution.py:27
  190.9 7.3 %all-to-all-start = ((s32[4,1,8]{2,1,0:T(1,128)}), s32[4,1,8]{2,1,0:T(1,128)S(1)}, u32[]{:S(2)}, u32[]{:S(2)}) async-start(s32[4,1,8]{2,1,0:T(1,128)} %bitcast.1), calls=%async_computation | async-start | bytes 4096 | tf_op jit(solution)/shard_map/all_to_all | solution.py:106
  199.5 18.1 %collective-permute-start.1 = (bf16[1,8,16384]{2,1,0:T(8,128)(2,1)S(1)}, bf16[1,8,16384]{2,1,0:T(8,128)(2,1)S(1)}, u32[]{:S(2)}, u32[]{:S(2)}) collective-permute-start(bf16[1,8,16384]{2,1,0:T(8,128)(2,1)S(1)} %get-tuple-element.8), channel_id=1, source_target_pairs={{0,8},{4,12},{8,0},{12,4},{1,9},{5,13},{9,1},{13,5},{2,10},{6,14},... | collective-permute-start | bytes 786440 | tf_op jit(solution)/shard_map/ppermute | solution.py:27
  201.9 22.2 %collective-permute-start.2 = (bf16[1,8,16384]{2,1,0:T(8,128)(2,1)S(1)}, bf16[1,8,16384]{2,1,0:T(8,128)(2,1)S(1)}, u32[]{:S(2)}, u32[]{:S(2)}) collective-permute-start(bf16[1,8,16384]{2,1,0:T(8,128)(2,1)S(1)} %get-tuple-element.7), channel_id=1, source_target_pairs={{0,12},{4,8},{8,4},{12,0},{1,13},{5,9},{9,5},{13,1},{2,14},{6,10},... | collective-permute-start | bytes 786440 | tf_op jit(solution)/shard_map/ppermute | solution.py:27
  224.5 3.4 %collective-permute-start.3 = (bf16[16,128,128]{2,1,0:T(8,128)(2,1)S(1)}, bf16[16,128,128]{2,1,0:T(8,128)(2,1)S(1)}, u32[]{:S(2)}, u32[]{:S(2)}) collective-permute-start(bf16[16,128,128]{2,1,0:T(8,128)(2,1)S(1)} %bitcast.31), channel_id=1, source_target_pairs={{0,1},{1,0},{2,3},{3,2},{4,5},{5,4},{6,7},{7,6},{8,9},{9,8},{10,11... | collective-permute-start | bytes 1572872 | tf_op jit(solution)/shard_map/ppermute | solution.py:39
  224.6 5.3 %copy-start.1 = (bf16[512,4096]{1,0:T(8,128)(2,1)S(1)}, bf16[512,4096]{1,0:T(8,128)(2,1)}, u32[]{:S(2)}) copy-start(bf16[512,4096]{1,0:T(8,128)(2,1)} %all-gather.3.cloned.1.call-done) | copy-start | bytes 12582916
  224.6 5.3 %copy-start.2 = (bf16[4096,128]{1,0:T(8,128)(2,1)S(1)}, bf16[4096,128]{1,0:T(8,128)(2,1)}, u32[]{:S(2)}) copy-start(bf16[4096,128]{1,0:T(8,128)(2,1)} %param.10) | copy-start | bytes 3145732
  228.0 6.3 %collective-permute-start.4 = (bf16[256,128]{1,0:T(8,128)(2,1)S(1)}, bf16[256,128]{1,0:T(8,128)(2,1)S(1)}, u32[]{:S(2)}, u32[]{:S(2)}) collective-permute-start(bf16[256,128]{1,0:T(8,128)(2,1)S(1)} %bitcast.39), channel_id=1, source_target_pairs={{0,4},{4,8},{8,12},{1,5},{5,9},{9,13},{2,6},{6,10},{10,14},{3,7},{... | collective-permute-start | bytes 196616 | tf_op jit(solution)/shard_map/ppermute | solution.py:45
  231.3 6.3 %collective-permute-start.5 = (bf16[256,128]{1,0:T(8,128)(2,1)S(1)}, bf16[256,128]{1,0:T(8,128)(2,1)S(1)}, u32[]{:S(2)}, u32[]{:S(2)}) collective-permute-start(bf16[256,128]{1,0:T(8,128)(2,1)S(1)} %bitcast.40), channel_id=1, source_target_pairs={{0,4},{4,8},{8,12},{1,5},{5,9},{9,13},{2,6},{6,10},{10,14},{3,7},{... | collective-permute-start | bytes 196616 | tf_op jit(solution)/shard_map/ppermute | solution.py:45
Sparse Core Ops, SparseCore 0:
  8.9 155.8 all-gather.4
  166.4 34.4 all-gather.2
